TPU v7x, 32 devices: a whole 2x2x4 slice. The times are simulated.
32 devices in a mesh: pb: 4 (over y, core), col: 8 (over z, x).
Axes of the slice: x: 2, y: 2, z: 4, core: 2. Of those that a mesh axis runs over, the one named last changes fastest.
Arguments:
- queries: bfloat16 [2048, 1024], P(('pb', 'col')), may hold values from -6 to 6
- weights: bfloat16 [128, 512, 1024], P(('pb', 'col')), may hold values from -0.1875 to 0.1875
- shortlist: int32 [2048, 16], P(('pb', 'col')), may hold values from 0 to 127, all different within a row; in each aligned block of 64 rows (0 to 63, 64 to 127, ...) at most 24 rows name the same one
- pos_rank: int32 [2048, 4], P(('pb', 'col')), may hold values from 0 to 15
- pos_label: int32 [2048, 4], P(('pb', 'col')), may hold values from 0 to 511
Outputs:
- grad_weights: bfloat16 [128, 512, 1024], P(('pb', 'col'))
- grad_queries: bfloat16 [2048, 1024], P(('pb', 'col'))
Inputs may be any that keep to these rules, and one draw needn't show every extreme that they name: `shortlist`: each row names 16 different clusters. Among the 64 rows of one device no cluster is named more than 24 times, a bound that some block reaches.
All inputs are finite; a program needn't handle non-finite values.
Results may differ from a plain program's by a relative error of at most 0.012.
Values may be sent and summed in bfloat16 or wider, within the bound.
A program may use at most 128 MiB of HBM per device.

v0:
```python
import jax
import jax.numpy as jnp
from jax import lax
from jax.sharding import PartitionSpec as P


def pair_ranks(clusters_of):
    count = clusters_of.shape[0]
    same = clusters_of[:, None] == clusters_of[None, :]
    earlier = lax.broadcasted_iota(jnp.int32, (count, count), 1) < lax.broadcasted_iota(
        jnp.int32, (count, count), 0
    )
    return jnp.sum(jnp.logical_and(same, earlier), axis=1)


def place(
    rows_in, short_ids, rank_ids, label_ids, first_cluster, span_clusters, capacity, label_count
):
    query_rows, row_width = rows_in.shape
    top_count = short_ids.shape[1]
    clusters_of = short_ids.reshape(-1)
    ranks = pair_ranks(clusters_of)
    local_cluster = clusters_of - first_cluster
    inside = jnp.logical_and(local_cluster >= 0, local_cluster < span_clusters)
    slot_index = jnp.where(inside, local_cluster * capacity + ranks, span_clusters * capacity)
    total_slots = span_clusters * capacity
    repeated = jnp.broadcast_to(rows_in[:, None, :], (query_rows, top_count, row_width)).reshape(
        -1, row_width
    )
    filled = (
        jnp.zeros((total_slots, row_width), jnp.bfloat16).at[slot_index].set(repeated, mode="drop")
    )
    live_slots = (
        jnp.zeros((total_slots,), jnp.bfloat16)
        .at[slot_index]
        .set(jnp.ones((slot_index.shape[0],), jnp.bfloat16), mode="drop")
    )
    positions = lax.broadcasted_iota(jnp.int32, (1, top_count, 1), 1)
    matches = rank_ids[:, None, :] == positions
    codes = jnp.where(matches, (label_ids - label_count // 2)[:, None, :], -2 * label_count)
    codes = codes.reshape(query_rows * top_count, -1).astype(jnp.float32).astype(jnp.bfloat16)
    target_codes = (
        jnp.full((total_slots, codes.shape[1]), -2 * label_count, jnp.bfloat16)
        .at[slot_index]
        .set(codes, mode="drop")
    )
    return (filled, live_slots, target_codes, slot_index)


def owner_terms(arrived_rows, arrived_live, arrived_codes, weights):
    label_count = weights.shape[1]
    scores = jnp.einsum(
        "abjcd,jld->abjcl", arrived_rows, weights, preferred_element_type=jnp.float32
    )
    label_values = jnp.arange(label_count, dtype=jnp.float32)
    codes_wide = arrived_codes.astype(jnp.float32) + label_count // 2
    target = jnp.zeros(scores.shape, jnp.float32)
    for which in range(codes_wide.shape[-1]):
        target = jnp.maximum(
            target, (codes_wide[..., which : which + 1] == label_values).astype(jnp.float32)
        )
    grads = (
        (jax.nn.sigmoid(scores) - target) * arrived_live.astype(jnp.float32)[..., None]
    ).astype(jnp.bfloat16)
    grad_block = jnp.einsum(
        "abjcl,abjcd->jld", grads, arrived_rows, preferred_element_type=jnp.float32
    ).astype(jnp.bfloat16)
    part = jnp.einsum(
        "abjcl,jld->abjcd", grads, weights, preferred_element_type=jnp.float32
    ).astype(jnp.bfloat16)
    return (grad_block, part)


def body(queries, weights, shortlist, pos_rank, pos_label):
    query_rows, row_width = queries.shape
    owned_count, label_count, _ = weights.shape
    top_count = shortlist.shape[1]
    pb_count = lax.axis_size("pb")
    col_count = lax.axis_size("col")
    total_clusters = owned_count * pb_count * col_count
    capacity = 3 * query_rows * top_count // total_clusters
    grid_shape = (pb_count, col_count, owned_count, capacity)
    filled, live_slots, target_codes, slot_index = place(
        queries, shortlist, pos_rank, pos_label, 0, total_clusters, capacity, label_count
    )
    arrived = (
        lax.all_to_all(
            lax.all_to_all(
                filled.reshape(grid_shape + (row_width,)),
                "pb",
                split_axis=0,
                concat_axis=0,
                tiled=True,
            ),
            "col",
            split_axis=1,
            concat_axis=1,
            tiled=True,
        ),
        lax.all_to_all(
            lax.all_to_all(
                live_slots.reshape(grid_shape), "pb", split_axis=0, concat_axis=0, tiled=True
            ),
            "col",
            split_axis=1,
            concat_axis=1,
            tiled=True,
        ),
        lax.all_to_all(
            lax.all_to_all(
                target_codes.reshape(grid_shape + (-1,)),
                "pb",
                split_axis=0,
                concat_axis=0,
                tiled=True,
            ),
            "col",
            split_axis=1,
            concat_axis=1,
            tiled=True,
        ),
    )
    grad_weights, part = owner_terms(arrived[0], arrived[1], arrived[2], weights)
    returned = lax.all_to_all(
        lax.all_to_all(part, "pb", split_axis=0, concat_axis=0, tiled=True),
        "col",
        split_axis=1,
        concat_axis=1,
        tiled=True,
    )
    gathered_parts = jnp.take(returned.reshape(-1, row_width), slot_index, axis=0)
    grad_queries = jnp.sum(
        gathered_parts.reshape(query_rows, top_count, row_width), axis=1, dtype=jnp.float32
    ).astype(jnp.bfloat16)
    return (grad_weights, grad_queries)


def solution(mesh):
    return jax.shard_map(
        body,
        mesh=mesh,
        in_specs=(
            P(("pb", "col"), None),
            P(("pb", "col"), None, None),
            P(("pb", "col"), None),
            P(("pb", "col"), None),
            P(("pb", "col"), None),
        ),
        out_specs=(P(("pb", "col"), None, None), P(("pb", "col"), None)),
        check_vma=False,
    )
```

profile of v0, /device:TPU:0, one launch (start us, length us, event | category | flops | bytes accessed | tf_op | source)
XLA Modules:
  0.0 533.0 jit_solution(9637265200561461329)
XLA Ops:
  0.6 0.8 copy.80
  1.4 0.1 eq.95
  1.5 0.5 convert_reduce_fusion
  2.0 0.1 reduce_sum.27
  2.1 0.1 mul.29
  2.2 0.1 and.28
  2.3 7.6 %scatter_custom_fusion.2 = bf16[3072]{0:T(1024)(128)(2,1)S(1)} fusion(s32[1024]{0:T(1024)S(1)} %bitcast.67, bf16[1024]{0:T(1024)(128)(2,1)S(1)} %broadcast.106, bf16[]{:T(256)} %constant.15.clone.1), kind=kCustom, calls=%fused_computation.41 | custom fusion | bytes 6146 | tf_op jit(solution)/shard_map/scatter | solution.py:36
  9.9 0.1 reshape.104
  10.0 0.7 reshape.146
  10.7 4.3 all-to-all-start.4
  15.0 0.7 broadcast_add_fusion
  15.7 0.1 eq.102
  15.8 0.1 broadcast_in_dim.65
  15.9 0.1 broadcast_in_dim.66
  16.0 0.8 eq.99
  16.8 0.1 eq.100
  16.9 1.9 all-to-all-done.4
  18.8 0.1 reshape.147
  18.9 0.7 reshape.148
  19.7 6.2 %all-to-all-start.5 = ((bf16[8,2,192]{2,1,0:T(2,128)(2,1)}), bf16[8,2,192]{2,1,0:T(2,128)(2,1)S(1)}, u32[]{:S(2)}, u32[]{:S(2)}) async-start(bf16[8,2,192]{2,1,0:T(2,128)(2,1)} %reshape.148), calls=%async_computation.5 | async-start | bytes 16384 | tf_op jit(solution)/shard_map/all_to_all | solution.py:100
  25.9 0.2 copy.87
  26.1 3.4 scatter_custom_fusion.1
  29.6 1.0 copy.89
  30.6 0.8 reshape.150
  31.3 1.1 all-to-all-done.5
  32.4 3.4 all-to-all-start.2
  35.9 1.2 broadcast_in_dim.63
  37.0 9.1 %scatter_custom_fusion = bf16[3072,1024]{1,0:T(8,128)(2,1)} fusion(s32[1024]{0:T(1024)S(1)} %bitcast.69, bf16[1024,1024]{1,0:T(8,128)(2,1)S(1)} %bitcast.62, bf16[]{:T(256)} %constant.15.clone.1), kind=kCustom, calls=%fused_computation.24 | custom fusion | bytes 6291458 | tf_op jit(solution)/shard_map/scatter | solution.py:31
  46.1 6.5 %copy.84 = bf16[4,8,4,24,1024]{4,3,1,2,0:T(8,128)(2,1)} copy(bf16[4,8,4,24,1024]{4,3,2,1,0:T(8,128)(2,1)} %bitcast.60) | data formatting | bytes 12582912 | tf_op jit(solution)/shard_map/reshape | solution.py:89
  52.7 0.0 all-to-all-done.2
  52.7 5.2 all-to-all-start
  57.9 0.2 reshape.151
  58.2 0.8 reshape.152
  59.0 69.6 %all-to-all-done = bf16[4,8,4,24,1024]{4,3,1,2,0:T(8,128)(2,1)} async-done(((bf16[4,8,4,24,1024]{4,3,1,2,0:T(8,128)(2,1)}), bf16[4,8,4,24,1024]{4,3,1,2,0:T(8,128)(2,1)}, u32[]{:S(2)}, u32[]{:S(2)}) %all-to-all-start) | async-done | bytes 6291488 | tf_op jit(solution)/shard_map/all_to_all | solution.py:88
  128.6 4.9 all-to-all-start.3
  133.5 6.5 %copy.85 = bf16[4,8,4,24,1024]{4,3,0,2,1:T(8,128)(2,1)} copy(bf16[4,8,4,24,1024]{4,3,1,2,0:T(8,128)(2,1)} %all-to-all-done) | data formatting | bytes 12582912 | tf_op jit(solution)/shard_map/all_to_all | solution.py:88
  140.0 0.2 all-to-all-done.3
  140.1 5.8 %all-to-all-start.1 = ((bf16[4,8,4,24,1024]{4,3,0,2,1:T(8,128)(2,1)}), bf16[4,8,4,24,1024]{4,3,0,2,1:T(8,128)(2,1)}, u32[]{:S(2)}, u32[]{:S(2)}) async-start(bf16[4,8,4,24,1024]{4,3,0,2,1:T(8,128)(2,1)} %copy.85), calls=%async_computation.1 | async-start | bytes 12582912 | tf_op jit(solution)/shard_map/all_to_all | solution.py:87
  146.0 0.1 reshape.149
  146.1 0.2 reshape.153
  146.3 0.1 convert_add_fusion
  146.5 136.9 %all-to-all-done.1 = bf16[4,8,4,24,1024]{4,3,0,2,1:T(8,128)(2,1)} async-done(((bf16[4,8,4,24,1024]{4,3,0,2,1:T(8,128)(2,1)}), bf16[4,8,4,24,1024]{4,3,0,2,1:T(8,128)(2,1)}, u32[]{:S(2)}, u32[]{:S(2)}) %all-to-all-start.1) | async-done | bytes 6291488 | tf_op jit(solution)/shard_map/all_to_all | solution.py:87
  283.4 0.0 copy-start
  283.4 9.1 %fusion.1 = bf16[4,8,4,24,512]{4,3,1,0,2:T(8,128)(2,1)S(1)} fusion(bf16[4,512,1024]{2,1,0:T(8,128)(2,1)} %param.6, bf16[4,8,4,24,1024]{4,3,0,2,1:T(8,128)(2,1)} %all-to-all-done.1, f32[4,8,4,24]{3,1,0,2:T(8,128)S(1)} %copy.94, f32[4,8,4,24]{3,1,0,2:T(8,128)S(1)} %copy.93, f32[4,8,4,24]{3,1,0,2:T(8,128)S(1)} %copy.92, f32[4,8,4,24]{3,1,0,2:T(8,128)S(1)} %copy.91, ...), kind=kOutput, calls=%fused_computation.7 | convolution fusion | flops 3249540096 | bytes 13686784 | tf_op jit(solution)/shard_map/abjcd,jld->abjcl/dot_general | solution.py:52
  292.5 0.0 copy-done
  292.5 0.0 copy-start.1
  292.5 3.7 convert_bitcast_fusion
  296.2 0.0 copy-done.1
  296.2 1.0 copy.100
  297.2 73.3 %all_to_all.40 = bf16[4,8,4,24,1024]{4,3,1,2,0:T(8,128)(2,1)S(1)} all-to-all(bf16[4,8,4,24,1024]{4,3,1,2,0:T(8,128)(2,1)S(1)} %copy.100), channel_id=1, replica_groups=mesh['pb'=4,'col'=8] {'pb'}, dimensions={0} | all-to-all | bytes 12582912 | tf_op jit(solution)/shard_map/all_to_all | solution.py:125
  370.5 3.3 copy.101
  373.8 5.0 all-to-all-start.7
  378.8 9.2 %bitcast_convert_fusion = bf16[4,512,1024]{2,1,0:T(8,128)(2,1)} fusion(bf16[4,8,4,24,1024]{4,3,0,2,1:T(8,128)(2,1)} %all-to-all-done.1, bf16[4,8,4,24,512]{4,3,1,0,2:T(8,128)(2,1)} %copy-done.1), kind=kOutput, calls=%fused_computation.4 | convolution fusion | flops 3223322624 | bytes 13631488 | tf_op jit(solution)/shard_map/abjcl,abjcd->jld/dot_general | solution.py:65
  388.0 128.6 %all-to-all-done.7 = bf16[4,8,4,24,1024]{4,3,0,2,1:T(8,128)(2,1)} async-done(((bf16[4,8,4,24,1024]{4,3,0,2,1:T(8,128)(2,1)}), bf16[4,8,4,24,1024]{4,3,0,2,1:T(8,128)(2,1)}, u32[]{:S(2)}, u32[]{:S(2)}) %all-to-all-start.7) | async-done | bytes 6291488 | tf_op jit(solution)/shard_map/all_to_all | solution.py:124
  516.6 6.5 %copy.102 = bf16[4,8,4,24,1024]{4,3,2,1,0:T(8,128)(2,1)} copy(bf16[4,8,4,24,1024]{4,3,0,2,1:T(8,128)(2,1)} %all-to-all-done.7) | data formatting | bytes 12582912 | tf_op jit(solution)/shard_map/all_to_all | solution.py:124
  523.1 8.6 %gather_fusion = bf16[1024,1024]{1,0:T(8,128)(2,1)S(1)} fusion(bf16[3072,1024]{1,0:T(8,128)(2,1)} %bitcast.59, s32[1024]{0:T(1024)S(1)} %broadcast_clamp_fusion), kind=kCustom, calls=%fused_computation | custom fusion | bytes 4198400 | tf_op jit(solution)/shard_map/jit(_take)/gather | solution.py:131
  531.6 1.4 select_reduce_fusion
  (14 shorter events, 0.3 us)
Async XLA Ops:
  10.7 8.1 %all-to-all-start.4 = ((bf16[4,2,384]{2,1,0:T(2,128)(2,1)}), bf16[4,2,384]{2,1,0:T(2,128)(2,1)S(1)}, u32[]{:S(2)}, u32[]{:S(2)}) async-start(bf16[4,2,384]{2,1,0:T(2,128)(2,1)} %reshape.146), calls=%async_computation.4 | async-start | bytes 12288 | tf_op jit(solution)/shard_map/all_to_all | solution.py:101
  19.7 12.8 %all-to-all-start.5 = ((bf16[8,2,192]{2,1,0:T(2,128)(2,1)}), bf16[8,2,192]{2,1,0:T(2,128)(2,1)S(1)}, u32[]{:S(2)}, u32[]{:S(2)}) async-start(bf16[8,2,192]{2,1,0:T(2,128)(2,1)} %reshape.148), calls=%async_computation.5 | async-start | bytes 16384 | tf_op jit(solution)/shard_map/all_to_all | solution.py:100
  32.4 20.2 %all-to-all-start.2 = ((bf16[4,2,1536]{2,1,0:T(2,128)(2,1)}), bf16[4,2,1536]{2,1,0:T(2,128)(2,1)S(1)}, u32[]{:S(2)}, u32[]{:S(2)}) async-start(bf16[4,2,1536]{2,1,0:T(2,128)(2,1)} %reshape.150), calls=%async_computation.2 | async-start | bytes 49152 | tf_op jit(solution)/shard_map/all_to_all | solution.py:110
  52.7 75.9 %all-to-all-start = ((bf16[4,8,4,24,1024]{4,3,1,2,0:T(8,128)(2,1)}), bf16[4,8,4,24,1024]{4,3,1,2,0:T(8,128)(2,1)}, u32[]{:S(2)}, u32[]{:S(2)}) async-start(bf16[4,8,4,24,1024]{4,3,1,2,0:T(8,128)(2,1)} %copy.84), calls=%async_computation | async-start | bytes 12582912 | tf_op jit(solution)/shard_map/all_to_all | solution.py:88
  128.6 11.6 %all-to-all-start.3 = ((bf16[8,2,768]{2,1,0:T(2,128)(2,1)}), bf16[8,2,768]{2,1,0:T(2,128)(2,1)S(1)}, u32[]{:S(2)}, u32[]{:S(2)}) async-start(bf16[8,2,768]{2,1,0:T(2,128)(2,1)} %reshape.152), calls=%async_computation.3 | async-start | bytes 49152 | tf_op jit(solution)/shard_map/all_to_all | solution.py:109
  140.1 143.2 %all-to-all-start.1 = ((bf16[4,8,4,24,1024]{4,3,0,2,1:T(8,128)(2,1)}), bf16[4,8,4,24,1024]{4,3,0,2,1:T(8,128)(2,1)}, u32[]{:S(2)}, u32[]{:S(2)}) async-start(bf16[4,8,4,24,1024]{4,3,0,2,1:T(8,128)(2,1)} %copy.85), calls=%async_computation.1 | async-start | bytes 12582912 | tf_op jit(solution)/shard_map/all_to_all | solution.py:87
  283.4 9.1 %copy-start = (bf16[4,512,1024]{2,1,0:T(8,128)(2,1)S(1)}, bf16[4,512,1024]{2,1,0:T(8,128)(2,1)}, u32[]{:S(2)}) copy-start(bf16[4,512,1024]{2,1,0:T(8,128)(2,1)} %param.6) | copy-start | bytes 12582916
  292.5 3.7 copy-start.1
  373.8 142.8 %all-to-all-start.7 = ((bf16[4,8,4,24,1024]{4,3,0,2,1:T(8,128)(2,1)}), bf16[4,8,4,24,1024]{4,3,0,2,1:T(8,128)(2,1)}, u32[]{:S(2)}, u32[]{:S(2)}) async-start(bf16[4,8,4,24,1024]{4,3,0,2,1:T(8,128)(2,1)} %copy.101), calls=%async_computation.7 | async-start | bytes 12582912 | tf_op jit(solution)/shard_map/all_to_all | solution.py:124
where the time goes:
time: 534 us; the launch traced here: 533 us
  waiting for transfers between devices  338 us (63%)
  blocking collectives  73.3 us (14%)
  local copies, waits for them, and re-layouts  61 us (11%)
  starting transfers between devices  35 us (7%)
  matrix products  22 us (4%)
    all_to_all x1, waiting for transfers between devices, body(): lax.all_to_all(lax.all_to_all(filled.reshape(grid_shape + (row_width,)),...  137 us
    all_to_all x1, waiting for transfers between devices, body(): lax.all_to_all(lax.all_to_all(part, 'pb', split_axis=0, concat_axis=0, ti...  129 us
    all_to_all x1, blocking collectives, body(): lax.all_to_all(part, 'pb', split_axis=0, concat_axis=0, tiled=True)  73.3 us
    all_to_all x1, waiting for transfers between devices, body(): lax.all_to_all(filled.reshape(grid_shape + (row_width,)), 'pb', split_axi...  69.6 us
  transfers between devices with their start and end apart: 7, of which 6 were waited for; matrix products, arithmetic and copies ran while one was open for 8% of the time, Pallas kernels for 0%

commit v1 on v0

v1 whole, which is shorter than its diff:
```python
import functools

import jax
import jax.numpy as jnp
from jax import lax
from jax.experimental import pallas as pl
from jax.experimental.pallas import tpu as pltpu
from jax.sharding import PartitionSpec as P

META = 128


def query_meta(shortlist, pos_rank, pos_label):
    top_count = shortlist.shape[1]
    rank_ids = lax.broadcasted_iota(jnp.int32, (1, 1, top_count), 2)
    chosen = jnp.sum(jnp.where(pos_rank[:, :, None] == rank_ids, shortlist[:, None, :], 0), axis=2)
    fields = [shortlist // 256, shortlist % 256, chosen // 256, chosen % 256]
    fields += [pos_label // 256, pos_label % 256]
    packed = jnp.concatenate(fields, axis=1)
    packed = jnp.pad(packed, ((0, 0), (0, META - packed.shape[1])))
    return packed.astype(jnp.float32).astype(jnp.bfloat16)


def gradient_block(meta, scores, first_cluster, owned, labels, top_count, positives):
    meta = meta.astype(jnp.float32)
    first = first_cluster.astype(jnp.float32)
    t, p = top_count, positives
    named = meta[:, :t] * 256.0 + meta[:, t : 2 * t] - first
    base = 2 * t
    at_cluster = meta[:, base : base + p] * 256.0 + meta[:, base + p : base + 2 * p] - first
    at_label = meta[:, base + 2 * p : base + 3 * p] * 256.0 + meta[:, base + 3 * p : base + 4 * p]
    places = (at_cluster * labels + at_label).astype(jnp.int32)
    label_ids = lax.broadcasted_iota(jnp.int32, (1, labels), 1)
    columns = []
    for j in range(owned):
        live = jnp.max((named == float(j)).astype(jnp.float32), axis=1, keepdims=True)
        hit = None
        for w in range(p):
            same = (places[:, w : w + 1] - j * labels) == label_ids
            hit = same if hit is None else jnp.logical_or(hit, same)
        part = scores[:, j * labels : (j + 1) * labels]
        sig = 0.5 * jnp.tanh(0.5 * part) + 0.5
        columns.append(((sig - hit.astype(jnp.float32)) * live).astype(jnp.bfloat16))
    return jnp.concatenate(columns, axis=1)


def dense_kernel(owned, labels, top_count, positives, q_ref, m_ref, w_ref, gw_ref, part_ref, acc):
    step = pl.program_id(0)
    me = lax.axis_index("pb") * lax.axis_size("col") + lax.axis_index("col")

    @pl.when(step == 0)
    def _():
        acc[...] = jnp.zeros_like(acc)

    q = q_ref[...]
    scores = lax.dot_general(q, w_ref[...], (((1,), (1,)), ((), ())), preferred_element_type=jnp.float32)
    g = gradient_block(m_ref[...], scores, me * owned, owned, labels, top_count, positives)
    part_ref[...] = jnp.dot(g, w_ref[...], preferred_element_type=jnp.float32).astype(jnp.bfloat16)
    acc[...] += lax.dot_general(g, q, (((0,), (0,)), ((), ())), preferred_element_type=jnp.float32)

    @pl.when(step == pl.num_programs(0) - 1)
    def _():
        gw_ref[...] = acc[...].astype(jnp.bfloat16)


def body(queries, weights, shortlist, pos_rank, pos_label):
    rows, width = queries.shape
    owned, labels, _ = weights.shape
    pb_count, col_count = lax.axis_size("pb"), lax.axis_size("col")
    devices = pb_count * col_count
    sent = jnp.concatenate([queries, query_meta(shortlist, pos_rank, pos_label)], axis=1)
    everyone = lax.all_gather(sent, ("pb", "col"), axis=0, tiled=True)
    total = devices * rows
    block = 256
    grad_weights, part = pl.pallas_call(
        functools.partial(dense_kernel, owned, labels, shortlist.shape[1], pos_rank.shape[1]),
        grid=(total // block,),
        in_specs=[
            pl.BlockSpec((block, width), lambda i: (i, 0)),
            pl.BlockSpec((block, META), lambda i: (i, width // META)),
            pl.BlockSpec((owned * labels, width), lambda i: (0, 0)),
        ],
        out_specs=[
            pl.BlockSpec((owned * labels, width), lambda i: (0, 0)),
            pl.BlockSpec((block, width), lambda i: (i, 0)),
        ],
        out_shape=[
            jax.ShapeDtypeStruct((owned * labels, width), jnp.bfloat16),
            jax.ShapeDtypeStruct((total, width), jnp.bfloat16),
        ],
        scratch_shapes=[pltpu.VMEM((owned * labels, width), jnp.float32)],
        compiler_params=pltpu.CompilerParams(vmem_limit_bytes=60 * 1024 * 1024),
    )(everyone, everyone, weights.reshape(owned * labels, width))
    part = part.reshape(pb_count, col_count, rows, width)
    part = lax.all_to_all(part, "pb", split_axis=0, concat_axis=0, tiled=True)
    part = jnp.sum(part, axis=0, dtype=jnp.float32).astype(jnp.bfloat16)
    part = lax.all_to_all(part, "col", split_axis=0, concat_axis=0, tiled=True)
    grad_queries = jnp.sum(part, axis=0, dtype=jnp.float32).astype(jnp.bfloat16)
    return grad_weights.reshape(weights.shape), grad_queries


def solution(mesh):
    return jax.shard_map(
        body,
        mesh=mesh,
        in_specs=(
            P(("pb", "col"), None),
            P(("pb", "col"), None, None),
            P(("pb", "col"), None),
            P(("pb", "col"), None),
            P(("pb", "col"), None),
        ),
        out_specs=(P(("pb", "col"), None, None), P(("pb", "col"), None)),
        check_vma=False,
    )
```

time: 534 us -> 214 us (0.40)
  waiting for transfers between devices: 338 us -> 66.5 us
  local copies, waits for them, and re-layouts: 61 us -> 1.76 us
  Pallas kernels: 0 us -> 42.2 us
  starting transfers between devices: 35 us -> 0.04 us
  matrix products: 22 us -> 0 us
  between operations: 0.9 us -> 14.1 us
  blocking collectives: 73.3 us -> 82.8 us
    all_to_all x7 -> x0, waiting for transfers between devices: 338 us -> none  [the longest x1 137 us: body(): lax.all_to_all(lax.all_to_all(filled.reshape(grid_shape + (row_width,)),...]
    all_gather x0 -> x1, waiting for transfers between devices: none -> 66.5 us  [body(): everyone = lax.all_gather(sent, ('pb', 'col'), axis=0, tiled=True)]
    pallas_call x0 -> x1, Pallas kernels: none -> 42.2 us  [body(): pl.pallas_call(functools.partial(dense_kernel, owned, labels, shortlist.s...]
    all_to_all x7 -> x0, starting transfers between devices: 35 us -> none  [the longest x1 6.24 us: body(): lax.all_to_all(lax.all_to_all(live_slots.reshape(grid_shape), 'pb', split...]
    dot_general x3 -> x0, matrix products: 22 us -> none  [the longest x1 9.21 us: owner_terms(): jnp.einsum('abjcl,abjcd->jld', grads, arrived_rows, preferred_element_typ...]
    scatter x3 -> x0, local copies, waits for them, and re-layouts: 20.1 us -> none  [the longest x1 9.1 us: place(): jnp.zeros((total_slots, row_width), jnp.bfloat16).at[slot_index]]
    all_to_all x4 -> x0, local copies, waits for them, and re-layouts: 16.3 us -> none  [the longest x1 6.49 us: body(): lax.all_to_all(lax.all_to_all(part, 'pb', split_axis=0, concat_axis=0, ti...]
    all_to_all x1 -> x2, blocking collectives: 73.3 us -> 82.8 us  [the longest x1 53.8 us: body(): part = lax.all_to_all(part, 'pb', split_axis=0, concat_axis=0, tiled=True)]
  transfers between devices with their start and end apart: 7 -> 1, of which waited for: 6 -> 1; matrix products, arithmetic and copies ran while one was open for 8% -> 0% of each run, Pallas kernels for 0% -> 0%
where the time goes in v1:
time: 214 us
  blocking collectives  82.8 us (39%)
  waiting for transfers between devices  66.5 us (31%)
  Pallas kernels  42.2 us (20%)
  between operations  14.1 us (7%)
  other arithmetic  6.52 us (3%)
    all_gather x1, waiting for transfers between devices, body(): everyone = lax.all_gather(sent, ('pb', 'col'), axis=0, tiled=True)  66.5 us
    all_to_all x1, blocking collectives, body(): part = lax.all_to_all(part, 'pb', split_axis=0, concat_axis=0, tiled=True)  53.8 us
    pallas_call x1, Pallas kernels, body(): pl.pallas_call(functools.partial(dense_kernel, owned, labels, shortlist.s...  42.2 us
    all_to_all x1, blocking collectives, body(): part = lax.all_to_all(part, 'col', split_axis=0, concat_axis=0, tiled=True)  29 us
  transfers between devices with their start and end apart: 1, of which 1 were waited for; matrix products, arithmetic and copies ran while one was open for 0% of the time, Pallas kernels for 0%

profile of v1, /device:TPU:0, one launch (start us, length us, event | category | flops | bytes accessed | tf_op | source)
XLA Modules:
  0.0 213.9 jit_solution(6988332811002693497)
XLA Ops:
  7.2 0.0 all-gather.2.cloned.1.call-start
  7.2 0.8 copy.17
  8.0 0.7 select_reduce_fusion
  8.7 0.1 copy.21
  8.8 0.8 copy.25
  9.6 0.1 add_select_fusion
  9.7 0.1 concatenate.6
  9.8 1.6 pad_maximum_fusion
  11.4 0.0 all-gather.2.cloned.1.call-update
  11.4 66.5 %all-gather.2.cloned.1.call-done.q_ref.m_ref = bf16[2048,1152]{1,0:T(8,128)(2,1)} async-done(((bf16[64,1152]{1,0:T(8,128)(2,1)}), bf16[2048,1152]{1,0:T(8,128)(2,1)}) %all-gather.2.cloned.1.call-update) | async-done | bytes 4718608 | tf_op jit(solution)/shard_map/all_gather | solution.py:72
  77.9 42.2 %shard_map.68 = (bf16[2048,1024]{1,0:T(8,128)(2,1)}, bf16[2048,1024]{1,0:T(8,128)(2,1)}) custom-call(bf16[2048,1152]{1,0:T(8,128)(2,1)} %all-gather.2.cloned.1.call-done.q_ref.m_ref, bf16[2048,1152]{1,0:T(8,128)(2,1)} %all-gather.2.cloned.1.call-done.q_ref.m_ref, bf16[2048,1024]{1,0:T(8,128)(2,1)} %bitcast.3), custom_call_target="tpu_custom_call" | custom-call | tf_op jit(solution)/shard_map/pallas_call | solution.py:75
  120.1 53.8 %all_to_all.10 = bf16[4,8,64,1024]{3,2,1,0:T(8,128)(2,1)} all-to-all(bf16[4,8,64,1024]{3,2,1,0:T(8,128)(2,1)} %bitcast.4), channel_id=1, replica_groups=mesh['pb'=4,'col'=8] {'pb'}, dimensions={0} | all-to-all | bytes 8388608 | tf_op jit(solution)/shard_map/all_to_all | solution.py:95
  173.9 3.3 %reduce_sum.34 = bf16[8,64,1024]{2,1,0:T(8,128)(2,1)S(1)} reduce(bf16[4,8,64,1024]{3,2,1,0:T(8,128)(2,1)} %all_to_all.10, bf16[]{:T(256)} %constant.61.clone.1), dimensions={0}, to_apply=%region_1.2 | reduce | flops 1572864 | bytes 5242882 | tf_op jit(solution)/shard_map/reduce_sum | solution.py:96
  177.2 29.0 %all_to_all.11 = bf16[8,64,1024]{2,1,0:T(8,128)(2,1)S(1)} all-to-all(bf16[8,64,1024]{2,1,0:T(8,128)(2,1)S(1)} %reduce_sum.34), channel_id=1, replica_groups=mesh['pb'=4,'col'=8] {'col'}, dimensions={0} | all-to-all | bytes 2097152 | tf_op jit(solution)/shard_map/all_to_all | solution.py:97
  206.2 0.8 reduce_sum.35
  (2 shorter events, 0.0 us)
Async XLA Ops:
  7.2 70.8 %all-gather.2.cloned.1.call-start = ((), (), s32[]{:S(2)}) async-start(), calls=%async_computation.2 | async-start | bytes 4866048 | tf_op jit(solution)/shard_map/all_gather | solution.py:72
Sparse Core Ops, SparseCore 0:
  11.5 66.3 all-gather.1

commit v2 on v1

--- a/solution.py
+++ b/solution.py
@@ -63,12 +63,309 @@
         gw_ref[...] = acc[...].astype(jnp.bfloat16)
 
 
+OWN, PAIR, NEAR_A, NEAR_B, PAIR_NEAR_A, PAIR_NEAR_B, FAR, PAIR_FAR = 0, 1, 2, 3, 5, 4, 6, 7
+ZS = 4
+
+
+def routed_kernel(
+    owned,
+    labels,
+    top_count,
+    positives,
+    sent_ref,
+    w_hbm,
+    gw_hbm,
+    gq_ref,
+    w_ref,
+    qbuf,
+    gbuf,
+    part,
+    from_pair,
+    from_b,
+    from_a,
+    from_z,
+    gwbuf,
+    send_sem,
+    recv_sem,
+    w_sem,
+    out_sem,
+):
+    rows, _ = sent_ref.shape
+    width = w_ref.shape[1]
+    pb, col = lax.axis_index("pb"), lax.axis_index("col")
+    y, core = pb // 2, pb % 2
+    z, x = col // 2, col % 2
+    pair = (y * 2 + (1 - core), col)
+    xa = x + (1 - core) * (1 - 2 * x)
+    ya = y + core * (1 - 2 * y)
+    xb = x + core * (1 - 2 * x)
+    yb = y + (1 - core) * (1 - 2 * y)
+    side_a = (ya * 2 + core, z * 2 + xa)
+    side_b = (yb * 2 + core, z * 2 + xb)
+    z_peers = [None] + [(pb, ((z + k) % ZS) * 2 + x) for k in range(1, ZS)]
+    z_rows = [pl.ds(pl.multiple_of(((z + ZS - k) % ZS) * rows, rows), rows) for k in range(ZS)]
+    z_goals = [pl.ds(pl.multiple_of(((z + k) % ZS) * rows, rows), rows) for k in range(ZS)]
+
+    load_w = pltpu.make_async_copy(w_hbm, w_ref, w_sem)
+    load_w.start()
+
+    barrier = pltpu.get_barrier_semaphore()
+    for peer in z_peers[1:] + [side_a, side_b, pair]:
+        pl.semaphore_signal(barrier, inc=1, device_id=peer, device_id_type=pl.DeviceIdType.MESH)
+    pl.semaphore_wait(barrier, ZS + 2)
+
+    def copy(index, src, dst, peer):
+        return pltpu.make_async_remote_copy(
+            src_ref=src,
+            dst_ref=dst,
+            send_sem=send_sem.at[index],
+            recv_sem=recv_sem.at[index],
+            device_id=peer,
+            device_id_type=pl.DeviceIdType.MESH,
+        )
+
+    def chunk(slot, k):
+        return qbuf.at[slot, z_rows[k]]
+
+    z_copies = [None] + [copy(k, sent_ref, chunk(OWN, 0), z_peers[k]) for k in range(1, ZS)]
+    z_arrivals = [None] + [copy(k, sent_ref, chunk(OWN, k), z_peers[k]) for k in range(1, ZS)]
+
+    def source(slot, k):
+        return sent_ref if slot == OWN and k == 0 else chunk(slot, k)
+
+    def hops(base, from_slot, to_slot, peer):
+        return [copy(base + k, source(from_slot, k), chunk(to_slot, k), peer) for k in range(ZS)]
+
+    own_a = hops(4, OWN, NEAR_A, side_a)
+    own_b = hops(8, OWN, NEAR_B, side_b)
+    own_pair = hops(12, OWN, PAIR, pair)
+    a_b = hops(16, NEAR_A, FAR, side_b)
+    a_pair = hops(20, NEAR_A, PAIR_NEAR_B, pair)
+    b_pair = hops(24, NEAR_B, PAIR_NEAR_A, pair)
+    far_pair = hops(28, FAR, PAIR_FAR, pair)
+
+    for k in range(1, ZS):
+        z_copies[k].start()
+    own_a[0].start()
+    own_b[0].start()
+    own_pair[0].start()
+    qbuf[OWN, z_rows[0], :] = sent_ref[...]
+
+    def relay_z(k):
+        z_arrivals[k].wait_recv()
+        own_a[k].start()
+        own_b[k].start()
+        own_pair[k].start()
+
+    def relay_a(k):
+        own_a[k].wait_recv()
+        a_b[k].start()
+        a_pair[k].start()
+
+    relay_z(1)
+    relay_a(0)
+    relay_z(3)
+    relay_a(1)
+    relay_z(2)
+    load_w.wait()
+
+    first = (pb * lax.axis_size("col") + col) * owned
+
+    def score_step(s, _):
+        @pl.when(s == PAIR)
+        def _():
+            for k in range(ZS):
+                own_pair[k].wait_recv()
+            relay_a(3)
+
+        @pl.when(s == NEAR_A)
+        def _():
+            relay_a(2)
+
+        @pl.when(s == NEAR_B)
+        def _():
+            for k in range(ZS):
+                own_b[k].wait_recv()
+                b_pair[k].start()
+
+        @pl.when(s == PAIR_NEAR_B)
+        def _():
+            for k in range(ZS):
+                a_pair[k].wait_recv()
+
+        @pl.when(s == PAIR_NEAR_A)
+        def _():
+            for k in range(ZS):
+                b_pair[k].wait_recv()
+
+        @pl.when(s == FAR)
+        def _():
+            for k in range(ZS):
+                a_b[k].wait_recv()
+                far_pair[k].start()
+
+        @pl.when(s == PAIR_FAR)
+        def _():
+            for k in range(ZS):
+                far_pair[k].wait_recv()
+
+        scores = lax.dot_general(
+            qbuf[s, :, :width], w_ref[...], (((1,), (1,)), ((), ())), preferred_element_type=jnp.float32
+        )
+        gbuf[s] = gradient_block(
+            qbuf[s, :, width:], scores, first, owned, labels, top_count, positives
+        )
+        return 0
+
+    lax.fori_loop(0, 8, score_step, 0)
+
+    back_pair = {
+        PAIR_FAR: copy(32, part.at[PAIR_FAR], from_pair.at[0], pair),
+        PAIR_NEAR_A: copy(33, part.at[PAIR_NEAR_A], from_pair.at[1], pair),
+        PAIR_NEAR_B: copy(34, part.at[PAIR_NEAR_B], from_pair.at[2], pair),
+        PAIR: copy(35, part.at[PAIR], from_pair.at[3], pair),
+    }
+    back_far = copy(36, part.at[FAR], from_b.at[0], side_b)
+    back_b = copy(37, part.at[NEAR_B], from_b.at[1], side_b)
+    back_a = copy(38, part.at[NEAR_A], from_a, side_a)
+    back_z = [None] + [
+        copy(38 + k, part.at[OWN, z_goals[k]], from_z.at[k - 1], z_peers[k]) for k in range(1, ZS)
+    ]
+
+    def add_to(slot, *arrived):
+        total = part[slot].astype(jnp.float32)
+        for ref in arrived:
+            total = total + ref[...].astype(jnp.float32)
+        part[slot] = total.astype(jnp.bfloat16)
+
+    def part_step(t, _):
+        slot = 7 - t
+        part[slot] = jnp.dot(gbuf[slot], w_ref[...], preferred_element_type=jnp.float32).astype(
+            jnp.bfloat16
+        )
+        for which, back in back_pair.items():
+
+            @pl.when(slot == which)
+            def _():
+                back.start()
+
+        @pl.when(slot == 5)
+        def _():
+            back_pair[PAIR_FAR].wait_recv()
+            add_to(FAR, from_pair.at[0])
+            back_far.start()
+
+        @pl.when(slot == 3)
+        def _():
+            back_pair[PAIR_NEAR_A].wait_recv()
+            add_to(NEAR_B, from_pair.at[1])
+            back_b.start()
+
+        @pl.when(slot == 1)
+        def _():
+            back_pair[PAIR_NEAR_B].wait_recv()
+            back_far.wait_recv()
+            add_to(NEAR_A, from_pair.at[2], from_b.at[0])
+            back_a.start()
+
+        return 0
+
+    lax.fori_loop(0, 8, part_step, 0)
+
+    tile = labels // 2
+
+    def out_copy(u):
+        return pltpu.make_async_copy(
+            gwbuf.at[u], gw_hbm.at[pl.ds(pl.multiple_of(u * tile, tile), tile)], out_sem.at[u]
+        )
+
+    def weight_step(u, _):
+        columns = pl.ds(pl.multiple_of(u * tile, tile), tile)
+        g = gbuf[:, :, columns].reshape(-1, tile)
+        q = qbuf[:, :, :width].reshape(-1, width)
+        gwbuf[u] = lax.dot_general(
+            g, q, (((0,), (0,)), ((), ())), preferred_element_type=jnp.float32
+        ).astype(jnp.bfloat16)
+        out_copy(u).start()
+
+        @pl.when(u == 2)
+        def _():
+            back_pair[PAIR].wait_recv()
+            back_b.wait_recv()
+            back_a.wait_recv()
+            add_to(OWN, from_pair.at[3], from_b.at[1], from_a)
+            for k in range(1, ZS):
+                back_z[k].start()
+
+        return 0
+
+    count = owned * labels // tile
+    lax.fori_loop(0, count, weight_step, 0)
+
+    total = part[OWN, z_rows[0], :].astype(jnp.float32)
+    for k in range(1, ZS):
+        back_z[k].wait_recv()
+        total = total + from_z[k - 1].astype(jnp.float32)
+    gq_ref[...] = total.astype(jnp.bfloat16)
+
+    everything = z_copies[1:] + own_a + own_b + own_pair + a_b + a_pair + b_pair + far_pair
+    everything += list(back_pair.values()) + [back_far, back_b, back_a] + back_z[1:]
+    for one in everything:
+        one.wait_send()
+    for u in range(count):
+        out_copy(u).wait()
+
+
+def routed(sent, weights, top_count, positives):
+    rows, packed = sent.shape
+    owned, labels, width = weights.shape
+    block = ZS * rows
+    count = owned * labels // (labels // 2)
+    bf16 = jnp.bfloat16
+    return pl.pallas_call(
+        functools.partial(routed_kernel, owned, labels, top_count, positives),
+        in_specs=[
+            pl.BlockSpec(memory_space=pltpu.VMEM),
+            pl.BlockSpec(memory_space=pl.ANY),
+        ],
+        out_specs=[
+            pl.BlockSpec(memory_space=pl.ANY),
+            pl.BlockSpec(memory_space=pltpu.VMEM),
+        ],
+        out_shape=[
+            jax.ShapeDtypeStruct((owned * labels, width), bf16),
+            jax.ShapeDtypeStruct((rows, width), bf16),
+        ],
+        scratch_shapes=[
+            pltpu.VMEM((owned * labels, width), bf16),
+            pltpu.VMEM((8, block, packed), bf16),
+            pltpu.VMEM((8, block, owned * labels), bf16),
+            pltpu.VMEM((8, block, width), bf16),
+            pltpu.VMEM((4, block, width), bf16),
+            pltpu.VMEM((2, block, width), bf16),
+            pltpu.VMEM((block, width), bf16),
+            pltpu.VMEM((ZS - 1, rows, width), bf16),
+            pltpu.VMEM((count, labels // 2, width), bf16),
+            pltpu.SemaphoreType.DMA((42,)),
+            pltpu.SemaphoreType.DMA((42,)),
+            pltpu.SemaphoreType.DMA,
+            pltpu.SemaphoreType.DMA((count,)),
+        ],
+        compiler_params=pltpu.CompilerParams(
+            collective_id=0, has_side_effects=True, vmem_limit_bytes=60 * 1024 * 1024
+        ),
+    )(sent, weights.reshape(owned * labels, width))
+
+
 def body(queries, weights, shortlist, pos_rank, pos_label):
     rows, width = queries.shape
     owned, labels, _ = weights.shape
     pb_count, col_count = lax.axis_size("pb"), lax.axis_size("col")
     devices = pb_count * col_count
     sent = jnp.concatenate([queries, query_meta(shortlist, pos_rank, pos_label)], axis=1)
+    if (pb_count, col_count) == (4, 2 * ZS):
+        grad_weights, grad_queries = routed(sent, weights, shortlist.shape[1], pos_rank.shape[1])
+        return grad_weights.reshape(weights.shape), grad_queries
     everyone = lax.all_gather(sent, ("pb", "col"), axis=0, tiled=True)
     total = devices * rows
     block = 256

time: 214 us -> 89 us (0.42)
  blocking collectives: 82.8 us -> 0 us
  waiting for transfers between devices: 66.5 us -> 0 us
  Pallas kernels: 42.2 us -> 78 us
  between operations: 14.1 us -> 0.68 us
  local copies, waits for them, and re-layouts: 1.76 us -> 7.09 us
  other arithmetic: 6.52 us -> 2.4 us
    all_to_all x2 -> x0, blocking collectives: 82.8 us -> none  [the longest x1 53.8 us: body(): part = lax.all_to_all(part, 'pb', split_axis=0, concat_axis=0, tiled=True)]
    all_gather x1 -> x0, waiting for transfers between devices: 66.5 us -> none  [body(): everyone = lax.all_gather(sent, ('pb', 'col'), axis=0, tiled=True)]
    pallas_call x1, Pallas kernels: 42.2 us -> 78 us  [routed(): pl.pallas_call(functools.partial(routed_kernel, owned, labels, top_count,...]
    unnamed x2 -> x6, local copies, waits for them, and re-layouts: 1.55 us -> 6.88 us
    reduce_sum x2 -> x0, other arithmetic: 4.12 us -> none  [the longest x1 3.27 us: body(): part = jnp.sum(part, axis=0, dtype=jnp.float32).astype(jnp.bfloat16)]
  transfers between devices with their start and end apart: 1 -> 0, of which waited for: 1 -> 0; matrix products, arithmetic and copies ran while one was open for 0% -> 0% of each run, Pallas kernels for 0% -> 0%
where the time goes in v2:
time: 89 us; the launch traced here: 88.2 us
  Pallas kernels  78 us (88%)
  local copies, waits for them, and re-layouts  7.09 us (8%)
  other arithmetic  2.4 us (3%)
    pallas_call x1, Pallas kernels, routed(): pl.pallas_call(functools.partial(routed_kernel, owned, labels, top_count,...  78 us
    unnamed x6, local copies, waits for them, and re-layouts  6.88 us

profile of v2, /device:TPU:0, one launch (start us, length us, event | category | flops | bytes accessed | tf_op | source)
XLA Modules:
  0.0 88.2 jit_solution(667881929694127046)
XLA Ops:
  0.6 0.7 select_reduce_fusion
  1.4 0.1 copy.21
  1.4 0.8 copy.25
  2.2 0.8 copy.17
  3.0 0.1 add_select_fusion
  3.1 0.1 concatenate.6
  3.2 1.6 %pad_maximum_fusion.sent_ref = bf16[64,1152]{1,0:T(8,128)(2,1)} fusion(bf16[64,128]{1,0:T(8,128)(2,1)S(1)} %convert_convert_fusion, bf16[64,1024]{1,0:T(8,128)(2,1)} %param.5), kind=kLoop, calls=%fused_computation | loop fusion | flops 294912 | bytes 294912 | tf_op jit(solution)/shard_map/concatenate | solution.py:365
  4.8 78.0 %shard_map.68 = (bf16[2048,1024]{1,0:T(8,128)(2,1)}, bf16[64,1024]{1,0:T(8,128)(2,1)}) custom-call(bf16[64,1152]{1,0:T(8,128)(2,1)} %pad_maximum_fusion.sent_ref, bf16[2048,1024]{1,0:T(8,128)(2,1)} %bitcast.2), custom_call_target="tpu_custom_call" | custom-call | tf_op jit(solution)/shard_map/pallas_call | solution.py:325
  82.8 0.0 copy-start
  82.8 4.7 %copy.31 = bf16[4,512,1024]{2,1,0:T(8,128)(2,1)} copy(bf16[4,512,1024]{2,1,0:T(8,128)(2,1)} %bitcast.3) | data formatting | bytes 8388608
  87.5 0.0 copy-done
  87.5 0.7 copy.32
  (2 shorter events, 0.0 us)
Async XLA Ops:
  82.8 4.7 %copy-start = (bf16[64,1024]{1,0:T(8,128)(2,1)S(1)}, bf16[64,1024]{1,0:T(8,128)(2,1)}, u32[]{:S(2)}) copy-start(bf16[64,1024]{1,0:T(8,128)(2,1)} %get-tuple-element.17) | copy-start | bytes 393220

commit v3 on v2

--- a/solution.py
+++ b/solution.py
@@ -67,12 +67,44 @@
 ZS = 4
 
 
+def packed_meta(short_ref, rank_ref, label_ref):
+    short, ranks, places = short_ref[...], rank_ref[...], label_ref[...]
+    top_count, rows = short.shape
+    count = ranks.shape[0]
+    standing = lax.broadcasted_iota(jnp.int32, short.shape, 0)
+    lines = []
+    for w in range(count):
+        mine = jnp.where(standing == ranks[w : w + 1], short, 0)
+        lines.append(jnp.sum(mine, axis=0, keepdims=True))
+    lines = [v >> 8 for v in lines] + [v & 255 for v in lines]
+    lines += [places[w : w + 1] >> 8 for w in range(count)]
+    lines += [places[w : w + 1] & 255 for w in range(count)]
+    extra_ids = lax.broadcasted_iota(jnp.int32, (len(lines), rows), 0)
+    extra = jnp.zeros((len(lines), rows), jnp.int32)
+    for i, line in enumerate(lines):
+        extra = jnp.where(extra_ids == i, line, extra)
+    rest = jnp.zeros((META - 2 * top_count - len(lines), rows), jnp.int32)
+    fields = jnp.concatenate([short >> 8, short & 255, extra, rest], axis=0)
+    row_ids = lax.broadcasted_iota(jnp.int32, (rows, rows), 0)
+    col_ids = lax.broadcasted_iota(jnp.int32, (rows, rows), 1)
+    same = (row_ids == col_ids).astype(jnp.float32).astype(jnp.bfloat16)
+    return lax.dot_general(
+        same,
+        fields.astype(jnp.float32).astype(jnp.bfloat16),
+        (((1,), (1,)), ((), ())),
+        preferred_element_type=jnp.float32,
+    ).astype(jnp.bfloat16)
+
+
 def routed_kernel(
     owned,
     labels,
     top_count,
     positives,
-    sent_ref,
+    q_ref,
+    short_ref,
+    rank_ref,
+    label_ref,
     w_hbm,
     gw_hbm,
     gq_ref,
@@ -90,8 +122,7 @@
     w_sem,
     out_sem,
 ):
-    rows, _ = sent_ref.shape
-    width = w_ref.shape[1]
+    rows, width = q_ref.shape
     pb, col = lax.axis_index("pb"), lax.axis_index("col")
     y, core = pb // 2, pb % 2
     z, x = col // 2, col % 2
@@ -102,9 +133,9 @@
     yb = y + (1 - core) * (1 - 2 * y)
     side_a = (ya * 2 + core, z * 2 + xa)
     side_b = (yb * 2 + core, z * 2 + xb)
-    z_peers = [None] + [(pb, ((z + k) % ZS) * 2 + x) for k in range(1, ZS)]
-    z_rows = [pl.ds(pl.multiple_of(((z + ZS - k) % ZS) * rows, rows), rows) for k in range(ZS)]
-    z_goals = [pl.ds(pl.multiple_of(((z + k) % ZS) * rows, rows), rows) for k in range(ZS)]
+    z_of = [z, z + 1 - 2 * (z % 2), (z + 2) % ZS, ZS - 1 - z]
+    z_peers = [(pb, zk * 2 + x) for zk in z_of]
+    z_rows = [pl.ds(pl.multiple_of(zk * rows, rows), rows) for zk in z_of]
 
     load_w = pltpu.make_async_copy(w_hbm, w_ref, w_sem)
     load_w.start()
@@ -112,6 +143,8 @@
     barrier = pltpu.get_barrier_semaphore()
     for peer in z_peers[1:] + [side_a, side_b, pair]:
         pl.semaphore_signal(barrier, inc=1, device_id=peer, device_id_type=pl.DeviceIdType.MESH)
+    qbuf[OWN, z_rows[0], :width] = q_ref[...]
+    qbuf[OWN, z_rows[0], width:] = packed_meta(short_ref, rank_ref, label_ref)
     pl.semaphore_wait(barrier, ZS + 2)
 
     def copy(index, src, dst, peer):
@@ -127,14 +160,15 @@
     def chunk(slot, k):
         return qbuf.at[slot, z_rows[k]]
 
-    z_copies = [None] + [copy(k, sent_ref, chunk(OWN, 0), z_peers[k]) for k in range(1, ZS)]
-    z_arrivals = [None] + [copy(k, sent_ref, chunk(OWN, k), z_peers[k]) for k in range(1, ZS)]
-
-    def source(slot, k):
-        return sent_ref if slot == OWN and k == 0 else chunk(slot, k)
+    z_copies = [None] + [
+        copy(k, chunk(OWN, 0), chunk(OWN, 0), z_peers[k]) for k in range(1, ZS)
+    ]
+    z_arrivals = [None] + [
+        copy(k, chunk(OWN, 0), chunk(OWN, k), z_peers[k]) for k in range(1, ZS)
+    ]
 
     def hops(base, from_slot, to_slot, peer):
-        return [copy(base + k, source(from_slot, k), chunk(to_slot, k), peer) for k in range(ZS)]
+        return [copy(base + k, chunk(from_slot, k), chunk(to_slot, k), peer) for k in range(ZS)]
 
     own_a = hops(4, OWN, NEAR_A, side_a)
     own_b = hops(8, OWN, NEAR_B, side_b)
@@ -144,12 +178,11 @@
     b_pair = hops(24, NEAR_B, PAIR_NEAR_A, pair)
     far_pair = hops(28, FAR, PAIR_FAR, pair)
 
-    for k in range(1, ZS):
+    for k in (1, 3, 2):
         z_copies[k].start()
     own_a[0].start()
     own_b[0].start()
     own_pair[0].start()
-    qbuf[OWN, z_rows[0], :] = sent_ref[...]
 
     def relay_z(k):
         z_arrivals[k].wait_recv()
@@ -171,106 +204,100 @@
 
     first = (pb * lax.axis_size("col") + col) * owned
 
-    def score_step(s, _):
-        @pl.when(s == PAIR)
-        def _():
-            for k in range(ZS):
-                own_pair[k].wait_recv()
-            relay_a(3)
-
-        @pl.when(s == NEAR_A)
-        def _():
-            relay_a(2)
-
-        @pl.when(s == NEAR_B)
-        def _():
-            for k in range(ZS):
-                own_b[k].wait_recv()
-                b_pair[k].start()
-
-        @pl.when(s == PAIR_NEAR_B)
-        def _():
-            for k in range(ZS):
-                a_pair[k].wait_recv()
-
-        @pl.when(s == PAIR_NEAR_A)
-        def _():
-            for k in range(ZS):
-                b_pair[k].wait_recv()
-
-        @pl.when(s == FAR)
-        def _():
-            for k in range(ZS):
-                a_b[k].wait_recv()
-                far_pair[k].start()
-
-        @pl.when(s == PAIR_FAR)
-        def _():
-            for k in range(ZS):
-                far_pair[k].wait_recv()
-
-        scores = lax.dot_general(
-            qbuf[s, :, :width], w_ref[...], (((1,), (1,)), ((), ())), preferred_element_type=jnp.float32
-        )
-        gbuf[s] = gradient_block(
-            qbuf[s, :, width:], scores, first, owned, labels, top_count, positives
-        )
-        return 0
-
-    lax.fori_loop(0, 8, score_step, 0)
-
+    halves = [pl.ds(h * (width // 2), width // 2) for h in range(2)]
     back_pair = {
         PAIR_FAR: copy(32, part.at[PAIR_FAR], from_pair.at[0], pair),
         PAIR_NEAR_A: copy(33, part.at[PAIR_NEAR_A], from_pair.at[1], pair),
         PAIR_NEAR_B: copy(34, part.at[PAIR_NEAR_B], from_pair.at[2], pair),
         PAIR: copy(35, part.at[PAIR], from_pair.at[3], pair),
     }
-    back_far = copy(36, part.at[FAR], from_b.at[0], side_b)
-    back_b = copy(37, part.at[NEAR_B], from_b.at[1], side_b)
-    back_a = copy(38, part.at[NEAR_A], from_a, side_a)
-    back_z = [None] + [
-        copy(38 + k, part.at[OWN, z_goals[k]], from_z.at[k - 1], z_peers[k]) for k in range(1, ZS)
+    back_b = copy(36, part.at[NEAR_B], from_b.at[1], side_b)
+    back_far = [
+        copy(37 + h, part.at[FAR, :, halves[h]], from_b.at[0, :, halves[h]], side_b)
+        for h in range(2)
     ]
-
-    def add_to(slot, *arrived):
-        total = part[slot].astype(jnp.float32)
+    back_a = [
+        copy(39 + h, part.at[NEAR_A, :, halves[h]], from_a.at[:, halves[h]], side_a)
+        for h in range(2)
+    ]
+    back_z = [
+        [
+            copy(
+                41 + 3 * h + k - 1,
+                part.at[OWN, z_rows[k], halves[h]],
+                from_z.at[k - 1, :, halves[h]],
+                z_peers[k],
+            )
+            for k in (1, 3, 2)
+        ]
+        for h in range(2)
+    ]
+
+    def add_to(slot, columns, *arrived):
+        total = part[slot, :, columns].astype(jnp.float32)
         for ref in arrived:
-            total = total + ref[...].astype(jnp.float32)
-        part[slot] = total.astype(jnp.bfloat16)
-
-    def part_step(t, _):
-        slot = 7 - t
-        part[slot] = jnp.dot(gbuf[slot], w_ref[...], preferred_element_type=jnp.float32).astype(
-            jnp.bfloat16
+            total = total + ref[:, columns].astype(jnp.float32)
+        part[slot, :, columns] = total.astype(jnp.bfloat16)
+
+    def score_step(s, _):
+        @pl.when(s == PAIR)
+        def _():
+            for k in range(ZS):
+                own_pair[k].wait_recv()
+            relay_a(3)
+
+        @pl.when(s == NEAR_A)
+        def _():
+            relay_a(2)
+
+        @pl.when(s == NEAR_B)
+        def _():
+            for k in range(ZS):
+                own_b[k].wait_recv()
+                b_pair[k].start()
+
+        @pl.when(s == PAIR_NEAR_B)
+        def _():
+            for k in range(ZS):
+                a_pair[k].wait_recv()
+
+        @pl.when(s == PAIR_NEAR_A)
+        def _():
+            for k in range(ZS):
+                b_pair[k].wait_recv()
+
+        @pl.when(s == FAR)
+        def _():
+            for k in range(ZS):
+                a_b[k].wait_recv()
+                far_pair[k].start()
+
+        @pl.when(s == PAIR_FAR)
+        def _():
+            for k in range(ZS):
+                far_pair[k].wait_recv()
+
+        scores = lax.dot_general(
+            qbuf[s, :, :width], w_ref[...], (((1,), (1,)), ((), ())), preferred_element_type=jnp.float32
         )
+        g = gradient_block(qbuf[s, :, width:], scores, first, owned, labels, top_count, positives)
+        gbuf[s] = g
+        part[s] = jnp.dot(g, w_ref[...], preferred_element_type=jnp.float32).astype(jnp.bfloat16)
         for which, back in back_pair.items():
 
-            @pl.when(slot == which)
+            @pl.when(s == which)
             def _():
                 back.start()
 
-        @pl.when(slot == 5)
-        def _():
-            back_pair[PAIR_FAR].wait_recv()
-            add_to(FAR, from_pair.at[0])
-            back_far.start()
-
-        @pl.when(slot == 3)
+        @pl.when(s == FAR)
         def _():
             back_pair[PAIR_NEAR_A].wait_recv()
-            add_to(NEAR_B, from_pair.at[1])
+            add_to(NEAR_B, pl.ds(0, width), from_pair.at[1])
             back_b.start()
 
-        @pl.when(slot == 1)
-        def _():
-            back_pair[PAIR_NEAR_B].wait_recv()
-            back_far.wait_recv()
-            add_to(NEAR_A, from_pair.at[2], from_b.at[0])
-            back_a.start()
-
         return 0
 
-    lax.fori_loop(0, 8, part_step, 0)
+    lax.fori_loop(0, 8, score_step, 0)
 
     tile = labels // 2
 
@@ -288,46 +315,65 @@
         ).astype(jnp.bfloat16)
         out_copy(u).start()
 
-        @pl.when(u == 2)
-        def _():
-            back_pair[PAIR].wait_recv()
-            back_b.wait_recv()
-            back_a.wait_recv()
-            add_to(OWN, from_pair.at[3], from_b.at[1], from_a)
-            for k in range(1, ZS):
-                back_z[k].start()
+        @pl.when(u == 0)
+        def _():
+            back_pair[PAIR_FAR].wait_recv()
+            for h in range(2):
+                add_to(FAR, halves[h], from_pair.at[0])
+                back_far[h].start()
+            back_pair[PAIR_NEAR_B].wait_recv()
+
+        for h in range(2):
+
+            @pl.when(u == 2 + h)
+            def _():
+                back_far[h].wait_recv()
+                add_to(NEAR_A, halves[h], from_pair.at[2], from_b.at[0])
+                back_a[h].start()
+
+            @pl.when(u == 4 + h)
+            def _():
+                if h == 0:
+                    back_pair[PAIR].wait_recv()
+                    back_b.wait_recv()
+                back_a[h].wait_recv()
+                add_to(OWN, halves[h], from_pair.at[3], from_b.at[1], from_a)
+                for one in back_z[h]:
+                    one.start()
 
         return 0
 
     count = owned * labels // tile
     lax.fori_loop(0, count, weight_step, 0)
 
-    total = part[OWN, z_rows[0], :].astype(jnp.float32)
-    for k in range(1, ZS):
-        back_z[k].wait_recv()
-        total = total + from_z[k - 1].astype(jnp.float32)
-    gq_ref[...] = total.astype(jnp.bfloat16)
+    for h in range(2):
+        total = part[OWN, z_rows[0], halves[h]].astype(jnp.float32)
+        for one in back_z[h]:
+            one.wait_recv()
+        for k in range(ZS - 1):
+            total = total + from_z[k, :, halves[h]].astype(jnp.float32)
+        gq_ref[:, halves[h]] = total.astype(jnp.bfloat16)
 
     everything = z_copies[1:] + own_a + own_b + own_pair + a_b + a_pair + b_pair + far_pair
-    everything += list(back_pair.values()) + [back_far, back_b, back_a] + back_z[1:]
+    everything += list(back_pair.values()) + [back_b] + back_far + back_a + back_z[0] + back_z[1]
     for one in everything:
         one.wait_send()
     for u in range(count):
         out_copy(u).wait()
 
 
-def routed(sent, weights, top_count, positives):
-    rows, packed = sent.shape
+def routed(queries, weights, shortlist, pos_rank, pos_label):
+    rows = queries.shape[0]
+    packed = queries.shape[1] + META
+    top_count, positives = shortlist.shape[1], pos_rank.shape[1]
     owned, labels, width = weights.shape
     block = ZS * rows
     count = owned * labels // (labels // 2)
     bf16 = jnp.bfloat16
     return pl.pallas_call(
         functools.partial(routed_kernel, owned, labels, top_count, positives),
-        in_specs=[
-            pl.BlockSpec(memory_space=pltpu.VMEM),
-            pl.BlockSpec(memory_space=pl.ANY),
-        ],
+        in_specs=[pl.BlockSpec(memory_space=pltpu.VMEM)] * 4
+        + [pl.BlockSpec(memory_space=pl.ANY)],
         out_specs=[
             pl.BlockSpec(memory_space=pl.ANY),
             pl.BlockSpec(memory_space=pltpu.VMEM),
@@ -346,15 +392,21 @@
             pltpu.VMEM((block, width), bf16),
             pltpu.VMEM((ZS - 1, rows, width), bf16),
             pltpu.VMEM((count, labels // 2, width), bf16),
-            pltpu.SemaphoreType.DMA((42,)),
-            pltpu.SemaphoreType.DMA((42,)),
+            pltpu.SemaphoreType.DMA((47,)),
+            pltpu.SemaphoreType.DMA((47,)),
             pltpu.SemaphoreType.DMA,
             pltpu.SemaphoreType.DMA((count,)),
         ],
         compiler_params=pltpu.CompilerParams(
             collective_id=0, has_side_effects=True, vmem_limit_bytes=60 * 1024 * 1024
         ),
-    )(sent, weights.reshape(owned * labels, width))
+    )(
+        queries,
+        shortlist.T,
+        pos_rank.T,
+        pos_label.T,
+        weights.reshape(owned * labels, width),
+    )
 
 
 def body(queries, weights, shortlist, pos_rank, pos_label):
@@ -362,10 +414,10 @@
     owned, labels, _ = weights.shape
     pb_count, col_count = lax.axis_size("pb"), lax.axis_size("col")
     devices = pb_count * col_count
+    if (pb_count, col_count) == (4, 2 * ZS):
+        grad_weights, grad_queries = routed(queries, weights, shortlist, pos_rank, pos_label)
+        return grad_weights.reshape(weights.shape), grad_queries
     sent = jnp.concatenate([queries, query_meta(shortlist, pos_rank, pos_label)], axis=1)
-    if (pb_count, col_count) == (4, 2 * ZS):
-        grad_weights, grad_queries = routed(sent, weights, shortlist.shape[1], pos_rank.shape[1])
-        return grad_weights.reshape(weights.shape), grad_queries
     everyone = lax.all_gather(sent, ("pb", "col"), axis=0, tiled=True)
     total = devices * rows
     block = 256

time: 89 us -> 82.9 us (0.931)
  other arithmetic: 2.4 us -> 0 us
  local copies, waits for them, and re-layouts: 7.09 us -> 5.34 us
  Pallas kernels: 78 us -> 76.8 us
    concatenate x1 -> x0, other arithmetic: 1.58 us -> none  [body(): jnp.concatenate([queries, query_meta(shortlist, pos_rank, pos_label)], ax...]
    unnamed x6 -> x4, local copies, waits for them, and re-layouts: 6.88 us -> 5.34 us
    pallas_call x1, Pallas kernels: 78 us -> 76.8 us  [routed(): pl.pallas_call(functools.partial(routed_kernel, owned, labels, top_count,...]
where the time goes in v3:
time: 82.9 us; the launch traced here: 82.8 us
  Pallas kernels  76.8 us (93%)
  local copies, waits for them, and re-layouts  5.34 us (6%)
    pallas_call x1, Pallas kernels, routed(): pl.pallas_call(functools.partial(routed_kernel, owned, labels, top_count,...  76.8 us
    unnamed x4, local copies, waits for them, and re-layouts  5.34 us

profile of v3, /device:TPU:0, one launch (start us, length us, event | category | flops | bytes accessed | tf_op | source)
XLA Modules:
  0.0 82.8 jit_solution(8221520232549836973)
XLA Ops:
  0.6 76.8 %shard_map.68 = (bf16[2048,1024]{1,0:T(8,128)(2,1)}, bf16[64,1024]{1,0:T(8,128)(2,1)}) custom-call(bf16[64,1024]{1,0:T(8,128)(2,1)} %q_ref.1, s32[16,64]{1,0:T(8,128)} %bitcast.7, s32[4,64]{1,0:T(4,128)} %bitcast.8, s32[4,64]{1,0:T(4,128)} %bitcast.9, bf16[2048,1024]{1,0:T(8,128)(2,1)} %bitcast.5), custom_call_target="tpu_custom_call" | custom-call | tf_op jit(solution)/shard_map/pallas_call | solution.py:373
  77.4 0.0 copy-start
  77.4 4.7 %copy.9 = bf16[4,512,1024]{2,1,0:T(8,128)(2,1)} copy(bf16[4,512,1024]{2,1,0:T(8,128)(2,1)} %bitcast.6) | data formatting | bytes 8388608
  82.1 0.0 copy-done
  82.1 0.7 copy.10
Async XLA Ops:
  77.4 4.7 %copy-start = (bf16[64,1024]{1,0:T(8,128)(2,1)S(1)}, bf16[64,1024]{1,0:T(8,128)(2,1)}, u32[]{:S(2)}) copy-start(bf16[64,1024]{1,0:T(8,128)(2,1)} %get-tuple-element.9) | copy-start | bytes 393220
